TPU v7x, 32 devices: a whole 2x2x4 slice. The times are simulated.
32 devices in a mesh: dp: 2 (over x), tm: 4 (over z), space: 4 (over y, core).
Axes of the slice: x: 2, y: 2, z: 4, core: 2. Of those that a mesh axis runs over, the one named last changes fastest.
Arguments:
- latent: bfloat16 [2, 12, 8, 104, 384], P('dp', 'tm', 'space'), may hold values from -16 to 16
- attn_gain: float32 [384], replicated, may hold values from 0.5 to 1.5
- w_query: bfloat16 [384, 384], replicated, may hold values from -1 to 1
- w_key: bfloat16 [384, 384], replicated, may hold values from -1 to 1
- w_value: bfloat16 [384, 384], replicated, may hold values from -0.3125 to 0.3125
- w_out: bfloat16 [384, 384], replicated, may hold values from -1.25 to 1.25
- conv_gain_first: float32 [384], replicated, may hold values from 0.5 to 1.5
- conv_first: bfloat16 [3, 3, 3, 384, 384], replicated, may hold values from -0.0625 to 0.0625
- conv_gain_second: float32 [384], replicated, may hold values from 0.5 to 1.5
- conv_second: bfloat16 [3, 3, 3, 384, 384], replicated, may hold values from -0.0625 to 0.0625
- student_in: bfloat16 [384, 384], replicated, may hold values from -0.3125 to 0.3125
- student_out: bfloat16 [384, 384], replicated, may hold values from -0.3125 to 0.3125
Outputs:
- teacher_out: bfloat16 [2, 12, 8, 104, 384], P('dp', 'tm', 'space')
- grad_in: float32 [384, 384], replicated
- grad_out: float32 [384, 384], replicated
All inputs are finite; a program needn't handle non-finite values.
Results may differ from a plain program's by a relative error of at most 0.007.
Values may be sent and summed in bfloat16 or wider, within the bound.
No kernel may reach another device: no remote copies, remote signals or barrier semaphores. Data moves between devices by JAX's collectives and lax.ppermute only.
A program may use at most 128 MiB of HBM per device.

v0:
```python
import jax
import jax.numpy as jnp
from jax import lax
from jax.sharding import PartitionSpec as P


def from_behind(value, axis, by):
    count = lax.axis_size(axis)
    pairs = [(i, i + by) for i in range(count) if 0 <= i + by < count]
    return lax.ppermute(value, axis, pairs)


def extended_2(block, sides, width):
    for axis, dim in sides:
        count = lax.axis_size(axis)
        forward = [(i, i + 1) for i in range(count - 1)]
        backward = [(target, source) for source, target in forward]
        low = lax.ppermute(
            lax.slice_in_dim(block, block.shape[dim] - width, None, axis=dim), axis, forward
        )
        high = lax.ppermute(lax.slice_in_dim(block, 0, width, axis=dim), axis, backward)
        block = jnp.concatenate([low, block, high], axis=dim)
    return block


def root_norm(values, gain):
    return values * lax.rsqrt(jnp.mean(values * values, axis=-1, keepdims=True) + 1e-06) * gain


def attend(queries, all_keys, all_values, scale):
    scores = (
        jnp.einsum("fqc,fkc->fqk", queries, all_keys, preferred_element_type=jnp.float32) * scale
    )
    maxima = jnp.max(scores, axis=-1, keepdims=True)
    expos = jnp.exp(scores - maxima)
    totals = jnp.sum(expos, axis=-1, keepdims=True)
    weights = expos.astype(jnp.bfloat16)
    summed = jnp.einsum("fqk,fkc->fqc", weights, all_values, preferred_element_type=jnp.float32)
    return (summed / totals).astype(jnp.bfloat16)


def causal_conv(activation, weight):
    frame_count, row_count, column_count, channels = activation.shape
    earlier = from_behind(activation[frame_count - 2 :], "tm", 1)
    extended = jnp.concatenate([earlier, activation], axis=0)
    extended = extended_2(extended, (("space", 1),), 1)
    extended = jnp.pad(extended, ((0, 0), (0, 0), (1, 1), (0, 0)))
    total = jnp.zeros((frame_count * row_count * column_count, channels), jnp.float32)
    for tap_time in range(3):
        for tap_row in range(3):
            for tap_col in range(3):
                window = extended[
                    tap_time : tap_time + frame_count,
                    tap_row : tap_row + row_count,
                    tap_col : tap_col + column_count,
                ]
                total = total + jnp.dot(
                    window.reshape(-1, channels),
                    weight[tap_time, tap_row, tap_col],
                    preferred_element_type=jnp.float32,
                )
    return total


def shards(
    latent,
    attn_gain,
    w_query,
    w_key,
    w_value,
    w_out,
    conv_gain_first,
    conv_first,
    conv_gain_second,
    conv_second,
    student_in,
    student_out,
):
    frames = latent[0]
    frame_count, row_count, column_count, channels = frames.shape
    per_frame = row_count * column_count
    tokens_local = frames.reshape(-1, channels)
    inputs_wide = tokens_local.astype(jnp.float32)
    normed = root_norm(inputs_wide, attn_gain).astype(jnp.bfloat16)
    queries = (
        jnp.dot(normed, w_query, preferred_element_type=jnp.float32)
        .astype(jnp.bfloat16)
        .reshape(frame_count, per_frame, channels)
    )
    scale = channels ** (-0.5)
    piece = lax.all_gather(
        normed.reshape(frame_count, per_frame, channels), "space", axis=1, tiled=True
    )
    rows_flat = piece.reshape(-1, channels)
    piece_keys = jnp.dot(rows_flat, w_key, preferred_element_type=jnp.float32).astype(jnp.bfloat16)
    piece_values = jnp.dot(rows_flat, w_value, preferred_element_type=jnp.float32).astype(
        jnp.bfloat16
    )
    stacked = jnp.stack([piece_keys.reshape(piece.shape), piece_values.reshape(piece.shape)])
    mixed = attend(queries, stacked[0], stacked[1], scale)
    attention_out = jnp.dot(mixed.reshape(-1, channels), w_out, preferred_element_type=jnp.float32)
    mid = (inputs_wide + attention_out).astype(jnp.bfloat16)
    mid_wide = mid.astype(jnp.float32)
    first_act = jax.nn.silu(root_norm(mid_wide, conv_gain_first)).astype(jnp.bfloat16)
    first_conv = causal_conv(
        first_act.reshape(frame_count, row_count, column_count, channels), conv_first
    )
    second_act = jax.nn.silu(root_norm(first_conv, conv_gain_second)).astype(jnp.bfloat16)
    second_conv = causal_conv(
        second_act.reshape(frame_count, row_count, column_count, channels), conv_second
    )
    teacher = (mid_wide + second_conv).astype(jnp.bfloat16)
    student_pre = jnp.dot(tokens_local, student_in, preferred_element_type=jnp.float32)
    student_hidden = jax.nn.silu(student_pre).astype(jnp.bfloat16)
    predicted = inputs_wide + jnp.dot(
        student_hidden, student_out, preferred_element_type=jnp.float32
    )
    error = predicted - teacher.astype(jnp.float32)
    token_total = (
        frame_count * per_frame * lax.axis_size("dp") * lax.axis_size("tm") * lax.axis_size("space")
    )
    signal = (error * lax.rsqrt(error * error + 0.0625) * token_total ** (-0.5)).astype(
        jnp.bfloat16
    )
    over_tokens = (((0,), (0,)), ((), ()))
    local_out = lax.dot_general(
        student_hidden, signal, over_tokens, preferred_element_type=jnp.float32
    )
    back = lax.dot_general(
        signal, student_out, (((1,), (1,)), ((), ())), preferred_element_type=jnp.float32
    )
    logistic = jax.nn.sigmoid(student_pre)
    back_pre = (back * logistic * (1.0 + student_pre * (1.0 - logistic))).astype(jnp.bfloat16)
    local_in = lax.dot_general(
        tokens_local, back_pre, over_tokens, preferred_element_type=jnp.float32
    )
    grad_in, grad_out = lax.psum((local_in, local_out), ("dp", "tm", "space"))
    return (teacher.reshape(latent.shape), grad_in, grad_out)


def solution(mesh):
    return jax.shard_map(
        shards,
        mesh=mesh,
        in_specs=(
            P("dp", "tm", "space", None, None),
            P(),
            P(),
            P(),
            P(),
            P(),
            P(),
            P(),
            P(),
            P(),
            P(),
            P(),
        ),
        out_specs=(P("dp", "tm", "space", None, None), P(), P()),
        check_vma=False,
    )
```

profile of v0, /device:TPU:0, one launch (start us, length us, event | category | flops | bytes accessed | tf_op | source)
XLA Modules:
  0.0 266.9 jit_solution(10811238338962035714)
XLA Ops:
  7.2 1.2 multiply_reduce_fusion.2
  8.6 2.0 multiply_convert_fusion.3
  10.7 1.7 convolution_convert_fusion.2
  12.4 22.6 %all-gather.2.cloned.1.call-done = bf16[3,832,384]{2,1,0:T(8,128)(2,1)} async-done(((bf16[3,208,384]{2,1,0:T(8,128)(2,1)}), bf16[3,832,384]{2,1,0:T(8,128)(2,1)}) %all-gather.2.cloned.1.call-update) | async-done | bytes 1916944 | tf_op jit(solution)/shard_map/all_gather | solution.py:91
  35.0 3.0 %convolution_convert_fusion.1 = bf16[2496,384]{1,0:T(8,128)(2,1)S(1)} fusion(bf16[2496,384]{1,0:T(8,128)(2,1)} %bitcast.304, bf16[384,384]{1,0:T(8,128)(2,1)S(1)} %copy-done), kind=kOutput, calls=%fused_computation.3 | convolution fusion | flops 737058816 | bytes 4128768 | tf_op jit(solution)/shard_map/dot_general | solution.py:95
  38.1 1.3 convolution_convert_fusion
  39.4 1.0 multiply_reduce_fusion
  40.4 0.6 fusion.1
  41.1 1.0 fusion.47
  42.1 0.6 fusion.54
  43.1 3.4 %collective-permute-start = (bf16[2,2,104,384]{3,2,1,0:T(8,128)(2,1)S(1)}, bf16[2,2,104,384]{3,2,1,0:T(8,128)(2,1)S(1)}, u32[]{:S(2)}, u32[]{:S(2)}) collective-permute-start(bf16[2,2,104,384]{3,2,1,0:T(8,128)(2,1)S(1)} %bitcast.381), channel_id=1, source_target_pairs={{0,4},{4,8},{8,12},{1,5},{5,9},{9,13},{2,6},{6,10},{10,14},{3,7},{... | collective-permute-start | bytes 958472 | tf_op jit(solution)/shard_map/ppermute | solution.py:10
  47.1 6.6 %collective-permute-done = bf16[2,2,104,384]{3,2,1,0:T(8,128)(2,1)S(1)} collective-permute-done((bf16[2,2,104,384]{3,2,1,0:T(8,128)(2,1)S(1)}, bf16[2,2,104,384]{3,2,1,0:T(8,128)(2,1)S(1)}, u32[]{:S(2)}, u32[]{:S(2)}) %collective-permute-start) | collective-permute-done | bytes 319520 | tf_op jit(solution)/shard_map/ppermute | solution.py:10
  53.8 1.3 collective-permute-start.1
  55.1 1.5 collective-permute-start.2
  57.7 1.8 collective-permute-done.2
  59.5 0.7 fusion.10
  60.2 2.6 fusion.226
  62.8 0.5 fusion.156
  63.8 0.5 fusion.163
  65.4 0.5 fusion.154
  66.4 0.5 fusion.151
  66.9 0.5 fusion.149
  67.9 0.5 fusion.142
  69.4 0.5 fusion.135
  69.9 0.5 fusion.133
  70.9 0.5 fusion.125
  71.4 0.5 fusion.123
  71.9 0.7 fusion.44
  72.6 0.5 fusion.42
  73.1 0.7 fusion.40
  73.8 0.5 fusion.35
  74.3 0.6 fusion.33
  75.0 0.5 fusion.31
  75.5 0.6 multiply_reduce_fusion.1
  76.5 4.7 %collective-permute-start.3 = (bf16[2,2,104,384]{3,2,1,0:T(8,128)(2,1)S(1)}, bf16[2,2,104,384]{3,2,1,0:T(8,128)(2,1)S(1)}, u32[]{:S(2)}, u32[]{:S(2)}) collective-permute-start(bf16[2,2,104,384]{3,2,1,0:T(8,128)(2,1)S(1)} %bitcast.380), channel_id=1, source_target_pairs={{0,4},{4,8},{8,12},{1,5},{5,9},{9,13},{2,6},{6,10},{10,14},{3,7},{... | collective-permute-start | bytes 958472 | tf_op jit(solution)/shard_map/ppermute | solution.py:10
  81.2 0.6 multiply_convert_fusion.1
  82.3 3.3 %collective-permute-done.3 = bf16[2,2,104,384]{3,2,1,0:T(8,128)(2,1)S(1)} collective-permute-done((bf16[2,2,104,384]{3,2,1,0:T(8,128)(2,1)S(1)}, bf16[2,2,104,384]{3,2,1,0:T(8,128)(2,1)S(1)}, u32[]{:S(2)}, u32[]{:S(2)}) %collective-permute-start.3) | collective-permute-done | bytes 319520 | tf_op jit(solution)/shard_map/ppermute | solution.py:10
  85.8 7.1 %collective-permute-start.4 = (bf16[5,1,104,384]{3,2,1,0:T(8,128)(2,1)S(1)}, bf16[5,1,104,384]{3,2,1,0:T(8,128)(2,1)S(1)}, u32[]{:S(2)}, u32[]{:S(2)}) collective-permute-start(bf16[5,1,104,384]{3,2,1,0:T(8,128)(2,1)S(1)} %get-tuple-element.60), channel_id=1, source_target_pairs={{0,1},{1,2},{2,3},{4,5},{5,6},{6,7},{8,9},{9,10},{10,11},{12,13},{... | collective-permute-start | bytes 1198088 | tf_op jit(solution)/shard_map/ppermute | solution.py:18
  92.9 1.3 collective-permute-start.5
  95.3 1.4 collective-permute-done.5
  96.7 0.7 select_maximum_fusion
  97.4 2.8 %fusion.225 = (bf16[3,2,104,384]{3,2,1,0:T(8,128)(2,1)S(1)}, bf16[3,2,104,384]{3,2,1,0:T(8,128)(2,1)S(1)}, bf16[3,2,104,384]{3,2,1,0:T(8,128)(2,1)S(1)}, bf16[3,...) fusion(bf16[5,4,106,384]{3,2,1,0:T(8,128)(2,1)S(1)} %select_max, ...), kind=kLoop, calls=%fused_computation.283 | loop fusion | bytes 17252352 | tf_op jit(solution)/shard_map/slice | solution.py:52
  101.2 0.5 fusion.116
  101.7 0.5 fusion.120
  102.6 0.5 fusion.107
  103.2 0.5 fusion.118
  104.2 0.5 fusion.102
  104.7 0.5 fusion.93
  106.2 0.5 fusion.91
  106.7 0.5 fusion.88
  107.8 0.5 fusion.83
  109.3 0.8 fusion.29
  110.0 0.5 fusion.27
  110.6 0.7 fusion.25
  111.2 0.6 fusion.20
  111.8 0.6 fusion.18
  112.4 0.5 fusion.16
  112.9 0.5 fusion.48
  113.5 0.7 multiply_convert_fusion
  114.1 1.3 fusion.231
  115.4 1.8 convolution_bitcast_fusion
  117.3 138.7 %all-reduce.5.cloned.1.call-done = (f32[384,384]{0,1:T(8,128)}, f32[384,384]{1,0:T(8,128)}) async-done(((f32[384,384]{0,1:T(8,128)}, f32[384,384]{1,0:T(8,128)}), (f32[384,384]{0,1:T(8,128)}, f32[384,384]{1,0:T(8,128)})) %all-reduce.5.cloned.1.call-update) | async-done | bytes 1179664 | tf_op jit(solution)/shard_map/psum | solution.py:137
  256.0 2.1 copy.15
  258.1 1.9 copy.18
  (77 shorter events, 13.1 us)
Async XLA Ops:
  7.2 27.9 %copy-start = (bf16[384,384]{1,0:T(8,128)(2,1)S(1)}, bf16[384,384]{1,0:T(8,128)(2,1)}, u32[]{:S(2)}) copy-start(bf16[384,384]{1,0:T(8,128)(2,1)} %param.15) | copy-start | bytes 884740
  7.2 27.9 %all-gather.2.cloned.1.call-start = ((), (), s32[]{:S(2)}) async-start(), calls=%async_computation | async-start | bytes 2396160 | tf_op jit(solution)/shard_map/all_gather | solution.py:91
  10.6 245.4 %all-reduce.5.cloned.1.call-start = ((), (), s32[]{:S(2)}) async-start(), calls=%async_computation.1 | async-start | bytes 2359296 | tf_op jit(solution)/shard_map/psum | solution.py:137
  12.4 25.6 %copy-start.5 = (bf16[384,384]{1,0:T(8,128)(2,1)S(1)}, bf16[384,384]{1,0:T(8,128)(2,1)}, u32[]{:S(2)}) copy-start(bf16[384,384]{1,0:T(8,128)(2,1)} %param.16) | copy-start | bytes 884740
  35.0 3.0 %copy-start.2 = (bf16[3,832,384]{2,1,0:T(8,128)(2,1)S(1)}, bf16[3,832,384]{2,1,0:T(8,128)(2,1)}, u32[]{:S(2)}) copy-start(bf16[3,832,384]{2,1,0:T(8,128)(2,1)} %all-gather.2.cloned.1.call-done) | copy-start | bytes 5750788
  39.4 7.2 %slice-start = ((s8[7962624]{0:T(1024)(128)(4,1)}), s8[4194304]{0:T(1024)(128)(4,1)S(1)}, s32[]{:S(2)}) async-start(s8[7962624]{0:T(1024)(128)(4,1)} %bitcast.315), calls=%async_computation.2 | async-start | bytes 8388608
  41.0 1.0 copy-start.3
  41.0 1.1 copy-start.8
  41.0 1.7 copy-start.6
  41.1 5.5 %slice-start.1 = ((s8[7962624]{0:T(1024)(128)(4,1)}), s8[3768320]{0:T(1024)(128)(4,1)S(1)}, s32[]{:S(2)}) async-start(s8[7962624]{0:T(1024)(128)(4,1)} %bitcast.315), calls=%async_computation.3 | async-start | bytes 7536640
  43.1 10.6 %collective-permute-start = (bf16[2,2,104,384]{3,2,1,0:T(8,128)(2,1)S(1)}, bf16[2,2,104,384]{3,2,1,0:T(8,128)(2,1)S(1)}, u32[]{:S(2)}, u32[]{:S(2)}) collective-permute-start(bf16[2,2,104,384]{3,2,1,0:T(8,128)(2,1)S(1)} %bitcast.381), channel_id=1, source_target_pairs={{0,4},{4,8},{8,12},{1,5},{5,9},{9,13},{2,6},{6,10},{10,14},{3,7},{... | collective-permute-start | bytes 958472 | tf_op jit(solution)/shard_map/ppermute | solution.py:10
  53.8 3.9 %collective-permute-start.1 = (bf16[5,1,104,384]{3,2,1,0:T(8,128)(2,1)S(1)}, bf16[5,1,104,384]{3,2,1,0:T(8,128)(2,1)S(1)}, u32[]{:S(2)}, u32[]{:S(2)}) collective-permute-start(bf16[5,1,104,384]{3,2,1,0:T(8,128)(2,1)S(1)} %get-tuple-element.66), channel_id=1, source_target_pairs={{0,1},{1,2},{2,3},{4,5},{5,6},{6,7},{8,9},{9,10},{10,11},{12,13},{... | collective-permute-start | bytes 1198088 | tf_op jit(solution)/shard_map/ppermute | solution.py:18
  55.1 4.4 %collective-permute-start.2 = (bf16[5,1,104,384]{3,2,1,0:T(8,128)(2,1)S(1)}, bf16[5,1,104,384]{3,2,1,0:T(8,128)(2,1)S(1)}, u32[]{:S(2)}, u32[]{:S(2)}) collective-permute-start(bf16[5,1,104,384]{3,2,1,0:T(8,128)(2,1)S(1)} %get-tuple-element.67), channel_id=1, source_target_pairs={{1,0},{2,1},{3,2},{5,4},{6,5},{7,6},{9,8},{10,9},{11,10},{13,12},{... | collective-permute-start | bytes 1198088 | tf_op jit(solution)/shard_map/ppermute | solution.py:21
  74.9 1.2 copy-start.7
  74.9 6.2 %copy-start.9 = (bf16[384,384]{1,0:T(8,128)(2,1)S(1)}, bf16[384,384]{1,0:T(8,128)(2,1)}, u32[]{:S(2)}) copy-start(bf16[384,384]{1,0:T(8,128)(2,1)} %param.22) | copy-start | bytes 884740
  74.9 6.8 %slice-start.2 = ((s8[7962624]{0:T(1024)(128)(4,1)}), s8[4194304]{0:T(1024)(128)(4,1)S(1)}, s32[]{:S(2)}) async-start(s8[7962624]{0:T(1024)(128)(4,1)} %bitcast.317), calls=%async_computation.4 | async-start | bytes 8388608
  75.5 6.3 %slice-start.3 = ((s8[7962624]{0:T(1024)(128)(4,1)}), s8[3768320]{0:T(1024)(128)(4,1)S(1)}, s32[]{:S(2)}) async-start(s8[7962624]{0:T(1024)(128)(4,1)} %bitcast.317), calls=%async_computation.5 | async-start | bytes 7536640
  76.5 9.1 %collective-permute-start.3 = (bf16[2,2,104,384]{3,2,1,0:T(8,128)(2,1)S(1)}, bf16[2,2,104,384]{3,2,1,0:T(8,128)(2,1)S(1)}, u32[]{:S(2)}, u32[]{:S(2)}) collective-permute-start(bf16[2,2,104,384]{3,2,1,0:T(8,128)(2,1)S(1)} %bitcast.380), channel_id=1, source_target_pairs={{0,4},{4,8},{8,12},{1,5},{5,9},{9,13},{2,6},{6,10},{10,14},{3,7},{... | collective-permute-start | bytes 958472 | tf_op jit(solution)/shard_map/ppermute | solution.py:10
  85.8 9.5 %collective-permute-start.4 = (bf16[5,1,104,384]{3,2,1,0:T(8,128)(2,1)S(1)}, bf16[5,1,104,384]{3,2,1,0:T(8,128)(2,1)S(1)}, u32[]{:S(2)}, u32[]{:S(2)}) collective-permute-start(bf16[5,1,104,384]{3,2,1,0:T(8,128)(2,1)S(1)} %get-tuple-element.60), channel_id=1, source_target_pairs={{0,1},{1,2},{2,3},{4,5},{5,6},{6,7},{8,9},{9,10},{10,11},{12,13},{... | collective-permute-start | bytes 1198088 | tf_op jit(solution)/shard_map/ppermute | solution.py:18
  92.9 3.8 %collective-permute-start.5 = (bf16[5,1,104,384]{3,2,1,0:T(8,128)(2,1)S(1)}, bf16[5,1,104,384]{3,2,1,0:T(8,128)(2,1)S(1)}, u32[]{:S(2)}, u32[]{:S(2)}) collective-permute-start(bf16[5,1,104,384]{3,2,1,0:T(8,128)(2,1)S(1)} %get-tuple-element.61), channel_id=1, source_target_pairs={{1,0},{2,1},{3,2},{5,4},{6,5},{7,6},{9,8},{10,9},{11,10},{13,12},{... | collective-permute-start | bytes 1198088 | tf_op jit(solution)/shard_map/ppermute | solution.py:21
  112.4 1.1 copy-start.10
  113.4 3.8 %copy-start.4 = (bf16[624,384]{1,0:T(8,128)(2,1)}, bf16[624,384]{1,0:T(8,128)(2,1)S(1)}, u32[]{:S(2)}) copy-start(bf16[624,384]{1,0:T(8,128)(2,1)S(1)} %fusion.48) | copy-start | bytes 1437700
  115.4 144.6 %copy-start.1 = (bf16[384,384]{1,0:T(8,128)(2,1)S(1)}, bf16[384,384]{1,0:T(8,128)(2,1)}, u32[]{:S(2)}) copy-start(bf16[384,384]{1,0:T(8,128)(2,1)} %param.15) | copy-start | bytes 884740
Sparse Core Ops, SparseCore 0:
  10.7 24.2 all-gather.1
  117.4 138.5 all-reduce.4
where the time goes:
time: 267 us
  waiting for transfers between devices  174 us (65%)
  matrix products  41 us (15%)
  starting transfers between devices  19.3 us (7%)
  between operations  14.7 us (6%)
  local copies, waits for them, and re-layouts  10.3 us (4%)
  other arithmetic  6.98 us (3%)
    psum x1, waiting for transfers between devices, shards(): grad_in, grad_out = lax.psum((local_in, local_out), ('dp', 'tm', 'space'))  139 us
    dot_general x54, matrix products, causal_conv(): jnp.dot(window.reshape(-1, channels), weight[tap_time, tap_row, tap_col],...  28.1 us
    all_gather x1, waiting for transfers between devices, shards(): lax.all_gather(normed.reshape(frame_count, per_frame, channels), 'space',...  22.6 us
    ppermute x2, waiting for transfers between devices, from_behind(): return lax.ppermute(value, axis, pairs)  9.94 us
    ppermute x2, starting transfers between devices, extended_2(): lax.ppermute(lax.slice_in_dim(block, block.shape[dim] - width, None, axis...  8.42 us
    ppermute x2, starting transfers between devices, from_behind(): return lax.ppermute(value, axis, pairs)  8.08 us
    slice x5, local copies, waits for them, and re-layouts, causal_conv(): extended[tap_time:tap_time + frame_count, tap_row:tap_row + row_count, ta...  5.87 us
  transfers between devices with their start and end apart: 8, of which 6 were waited for; matrix products, arithmetic and copies ran while one was open for 2% of the time, Pallas kernels for 0%

commit v1 on v0

--- a/solution.py
+++ b/solution.py
@@ -2,6 +2,18 @@
 import jax.numpy as jnp
 from jax import lax
 from jax.sharding import PartitionSpec as P
+
+
+def collect(array, axis, dim):
+    ways, here = (lax.axis_size(axis), lax.axis_index(axis))
+    grown, reach = (array, 1)
+    while reach < ways:
+        theirs = lax.ppermute(grown, axis, [(d, d ^ reach) for d in range(ways)])
+        mine_first = jnp.concatenate([grown, theirs], axis=dim)
+        theirs_first = jnp.concatenate([theirs, grown], axis=dim)
+        grown = jnp.where(here & reach == 0, mine_first, theirs_first)
+        reach = 2 * reach
+    return grown
 
 
 def from_behind(value, axis, by):
@@ -88,9 +100,7 @@
         .reshape(frame_count, per_frame, channels)
     )
     scale = channels ** (-0.5)
-    piece = lax.all_gather(
-        normed.reshape(frame_count, per_frame, channels), "space", axis=1, tiled=True
-    )
+    piece = collect(normed.reshape(frame_count, per_frame, channels), "space", 1)
     rows_flat = piece.reshape(-1, channels)
     piece_keys = jnp.dot(rows_flat, w_key, preferred_element_type=jnp.float32).astype(jnp.bfloat16)
     piece_values = jnp.dot(rows_flat, w_value, preferred_element_type=jnp.float32).astype(

time: 267 us -> 268 us (level)
  starting transfers between devices: 19.3 us -> 23.1 us
    all_gather x1 -> x0, waiting for transfers between devices: 22.6 us -> none  [shards(): lax.all_gather(normed.reshape(frame_count, per_frame, channels), 'space',...]
    ppermute x0 -> x2, waiting for transfers between devices: none -> 21.2 us  [collect(): theirs = lax.ppermute(grown, axis, [(d, d ^ reach) for d in range(ways)])]
    ppermute x0 -> x2, starting transfers between devices: none -> 3.5 us  [collect(): theirs = lax.ppermute(grown, axis, [(d, d ^ reach) for d in range(ways)])]
  transfers between devices with their start and end apart: 8 -> 9, of which waited for: 6 -> 7; matrix products, arithmetic and copies ran while one was open for 2% -> 2% of each run, Pallas kernels for 0% -> 0%
where the time goes in v1:
time: 268 us
  waiting for transfers between devices  173 us (65%)
  matrix products  39.4 us (15%)
  starting transfers between devices  23.1 us (9%)
  between operations  14.8 us (6%)
  local copies, waits for them, and re-layouts  10.3 us (4%)
  other arithmetic  7 us (3%)
    psum x1, waiting for transfers between devices, shards(): grad_in, grad_out = lax.psum((local_in, local_out), ('dp', 'tm', 'space'))  139 us
    dot_general x54, matrix products, causal_conv(): jnp.dot(window.reshape(-1, channels), weight[tap_time, tap_row, tap_col],...  28.1 us
    ppermute x2, waiting for transfers between devices, collect(): theirs = lax.ppermute(grown, axis, [(d, d ^ reach) for d in range(ways)])  21.2 us
    ppermute x2, waiting for transfers between devices, from_behind(): return lax.ppermute(value, axis, pairs)  9 us
    ppermute x2, starting transfers between devices, extended_2(): lax.ppermute(lax.slice_in_dim(block, block.shape[dim] - width, None, axis...  8.42 us
    ppermute x2, starting transfers between devices, from_behind(): return lax.ppermute(value, axis, pairs)  8.39 us
    slice x5, local copies, waits for them, and re-layouts, causal_conv(): extended[tap_time:tap_time + frame_count, tap_row:tap_row + row_count, ta...  5.87 us
  transfers between devices with their start and end apart: 9, of which 7 were waited for; matrix products, arithmetic and copies ran while one was open for 2% of the time, Pallas kernels for 0%

profile of v1, /device:TPU:0, one launch (start us, length us, event | category | flops | bytes accessed | tf_op | source)
XLA Modules:
  0.0 267.8 jit_solution(14751571623170421748)
XLA Ops:
  7.2 1.2 multiply_reduce_fusion.2
  8.6 1.2 multiply_convert_fusion.3
  9.8 0.6 collective-permute-start
  10.4 1.5 collective-permute-done
  12.2 2.9 %collective-permute-start.1 = (bf16[3,416,384]{2,1,0:T(8,128)(2,1)S(1)}, bf16[3,416,384]{2,1,0:T(8,128)(2,1)S(1)}, u32[]{:S(2)}, u32[]{:S(2)}) collective-permute-start(bf16[3,416,384]{2,1,0:T(8,128)(2,1)S(1)} %maximum_select_fusion.1), channel_id=1, source_target_pairs={{0,2},{1,3},{2,0},{3,1},{4,6},{5,7},{6,4},{7,5},{8,10},{9,11},{10,... | collective-permute-start | bytes 2875400 | tf_op jit(solution)/shard_map/ppermute | solution.py:11
  15.2 1.7 convolution_convert_fusion.2
  16.9 19.8 %collective-permute-done.1 = bf16[3,416,384]{2,1,0:T(8,128)(2,1)S(1)} collective-permute-done((bf16[3,416,384]{2,1,0:T(8,128)(2,1)S(1)}, bf16[3,416,384]{2,1,0:T(8,128)(2,1)S(1)}, u32[]{:S(2)}, u32[]{:S(2)}) %collective-permute-start.1) | collective-permute-done | bytes 958496 | tf_op jit(solution)/shard_map/ppermute | solution.py:11
  37.1 1.3 convolution_convert_fusion.1
  38.5 1.3 convolution_convert_fusion
  39.8 1.1 multiply_reduce_fusion
  40.9 0.6 fusion.1
  41.5 1.0 fusion.47
  42.6 0.6 fusion.54
  43.6 3.7 %collective-permute-start.2 = (bf16[2,2,104,384]{3,2,1,0:T(8,128)(2,1)S(1)}, bf16[2,2,104,384]{3,2,1,0:T(8,128)(2,1)S(1)}, u32[]{:S(2)}, u32[]{:S(2)}) collective-permute-start(bf16[2,2,104,384]{3,2,1,0:T(8,128)(2,1)S(1)} %bitcast.381), channel_id=1, source_target_pairs={{0,4},{4,8},{8,12},{1,5},{5,9},{9,13},{2,6},{6,10},{10,14},{3,7},{... | collective-permute-start | bytes 958472 | tf_op jit(solution)/shard_map/ppermute | solution.py:22
  47.8 5.7 %collective-permute-done.2 = bf16[2,2,104,384]{3,2,1,0:T(8,128)(2,1)S(1)} collective-permute-done((bf16[2,2,104,384]{3,2,1,0:T(8,128)(2,1)S(1)}, bf16[2,2,104,384]{3,2,1,0:T(8,128)(2,1)S(1)}, u32[]{:S(2)}, u32[]{:S(2)}) %collective-permute-start.2) | collective-permute-done | bytes 319520 | tf_op jit(solution)/shard_map/ppermute | solution.py:22
  53.6 1.3 collective-permute-start.3
  55.0 1.5 collective-permute-start.4
  57.6 2.7 %collective-permute-done.4 = bf16[5,1,104,384]{3,2,1,0:T(8,128)(2,1)S(1)} collective-permute-done((bf16[5,1,104,384]{3,2,1,0:T(8,128)(2,1)S(1)}, bf16[5,1,104,384]{3,2,1,0:T(8,128)(2,1)S(1)}, u32[]{:S(2)}, u32[]{:S(2)}) %collective-permute-start.4) | collective-permute-done | bytes 399392 | tf_op jit(solution)/shard_map/ppermute | solution.py:33
  60.3 0.7 fusion.10
  61.0 2.6 fusion.226
  63.6 0.5 fusion.156
  64.6 0.5 fusion.163
  66.1 0.5 fusion.154
  67.1 0.5 fusion.151
  67.6 0.5 fusion.149
  68.6 0.5 fusion.142
  70.1 0.5 fusion.135
  70.6 0.5 fusion.133
  71.6 0.5 fusion.125
  72.1 0.5 fusion.123
  72.6 0.7 fusion.44
  73.4 0.5 fusion.42
  73.9 0.7 fusion.40
  74.6 0.5 fusion.35
  75.1 0.6 fusion.33
  75.7 0.5 fusion.31
  76.3 0.6 multiply_reduce_fusion.1
  77.3 4.7 %collective-permute-start.5 = (bf16[2,2,104,384]{3,2,1,0:T(8,128)(2,1)S(1)}, bf16[2,2,104,384]{3,2,1,0:T(8,128)(2,1)S(1)}, u32[]{:S(2)}, u32[]{:S(2)}) collective-permute-start(bf16[2,2,104,384]{3,2,1,0:T(8,128)(2,1)S(1)} %bitcast.380), channel_id=1, source_target_pairs={{0,4},{4,8},{8,12},{1,5},{5,9},{9,13},{2,6},{6,10},{10,14},{3,7},{... | collective-permute-start | bytes 958472 | tf_op jit(solution)/shard_map/ppermute | solution.py:22
  82.0 0.6 multiply_convert_fusion.1
  83.1 3.3 %collective-permute-done.5 = bf16[2,2,104,384]{3,2,1,0:T(8,128)(2,1)S(1)} collective-permute-done((bf16[2,2,104,384]{3,2,1,0:T(8,128)(2,1)S(1)}, bf16[2,2,104,384]{3,2,1,0:T(8,128)(2,1)S(1)}, u32[]{:S(2)}, u32[]{:S(2)}) %collective-permute-start.5) | collective-permute-done | bytes 319520 | tf_op jit(solution)/shard_map/ppermute | solution.py:22
  86.5 7.1 %collective-permute-start.6 = (bf16[5,1,104,384]{3,2,1,0:T(8,128)(2,1)S(1)}, bf16[5,1,104,384]{3,2,1,0:T(8,128)(2,1)S(1)}, u32[]{:S(2)}, u32[]{:S(2)}) collective-permute-start(bf16[5,1,104,384]{3,2,1,0:T(8,128)(2,1)S(1)} %get-tuple-element.60), channel_id=1, source_target_pairs={{0,1},{1,2},{2,3},{4,5},{5,6},{6,7},{8,9},{9,10},{10,11},{12,13},{... | collective-permute-start | bytes 1198088 | tf_op jit(solution)/shard_map/ppermute | solution.py:30
  93.6 1.3 collective-permute-start.7
  96.1 1.4 collective-permute-done.7
  97.5 0.7 select_maximum_fusion
  98.2 2.8 %fusion.225 = (bf16[3,2,104,384]{3,2,1,0:T(8,128)(2,1)S(1)}, bf16[3,2,104,384]{3,2,1,0:T(8,128)(2,1)S(1)}, bf16[3,2,104,384]{3,2,1,0:T(8,128)(2,1)S(1)}, bf16[3,...) fusion(bf16[5,4,106,384]{3,2,1,0:T(8,128)(2,1)S(1)} %select_max, ...), kind=kLoop, calls=%fused_computation.285 | loop fusion | bytes 17252352 | tf_op jit(solution)/shard_map/slice | solution.py:64
  102.0 0.5 fusion.116
  102.5 0.5 fusion.120
  104.0 0.5 fusion.118
  105.5 0.5 fusion.93
  107.0 0.5 fusion.91
  108.5 0.5 fusion.83
  110.0 0.8 fusion.29
  110.8 0.5 fusion.27
  111.4 0.7 fusion.25
  112.0 0.6 fusion.20
  112.6 0.6 fusion.18
  113.2 0.5 fusion.16
  113.7 0.5 fusion.48
  114.2 0.7 multiply_convert_fusion
  114.9 1.3 fusion.231
  116.2 1.8 convolution_bitcast_fusion
  118.1 138.9 %all-reduce.5.cloned.1.call-done = (f32[384,384]{0,1:T(8,128)}, f32[384,384]{1,0:T(8,128)}) async-done(((f32[384,384]{0,1:T(8,128)}, f32[384,384]{1,0:T(8,128)}), (f32[384,384]{0,1:T(8,128)}, f32[384,384]{1,0:T(8,128)})) %all-reduce.5.cloned.1.call-update) | async-done | bytes 1179664 | tf_op jit(solution)/shard_map/psum | solution.py:147
  257.0 2.1 copy.15
  259.1 1.9 copy.18
  (78 shorter events, 15.3 us)
Async XLA Ops:
  7.2 30.0 %copy-start = (bf16[384,384]{1,0:T(8,128)(2,1)S(1)}, bf16[384,384]{1,0:T(8,128)(2,1)}, u32[]{:S(2)}) copy-start(bf16[384,384]{1,0:T(8,128)(2,1)} %param.15) | copy-start | bytes 884740
  7.2 249.8 %all-reduce.5.cloned.1.call-start = ((), (), s32[]{:S(2)}) async-start(), calls=%async_computation | async-start | bytes 2359296 | tf_op jit(solution)/shard_map/psum | solution.py:147
  9.8 2.0 collective-permute-start
  12.2 24.5 %collective-permute-start.1 = (bf16[3,416,384]{2,1,0:T(8,128)(2,1)S(1)}, bf16[3,416,384]{2,1,0:T(8,128)(2,1)S(1)}, u32[]{:S(2)}, u32[]{:S(2)}) collective-permute-start(bf16[3,416,384]{2,1,0:T(8,128)(2,1)S(1)} %maximum_select_fusion.1), channel_id=1, source_target_pairs={{0,2},{1,3},{2,0},{3,1},{4,6},{5,7},{6,4},{7,5},{8,10},{9,11},{10,... | collective-permute-start | bytes 2875400 | tf_op jit(solution)/shard_map/ppermute | solution.py:11
  37.1 1.4 copy-start.4
  39.8 7.5 %slice-start = ((s8[7962624]{0:T(1024)(128)(4,1)}), s8[4194304]{0:T(1024)(128)(4,1)S(1)}, s32[]{:S(2)}) async-start(s8[7962624]{0:T(1024)(128)(4,1)} %bitcast.315), calls=%async_computation.1 | async-start | bytes 8388608
  41.5 1.0 copy-start.2
  41.5 1.1 copy-start.7
  41.5 1.7 copy-start.5
  41.5 5.8 %slice-start.1 = ((s8[7962624]{0:T(1024)(128)(4,1)}), s8[3768320]{0:T(1024)(128)(4,1)S(1)}, s32[]{:S(2)}) async-start(s8[7962624]{0:T(1024)(128)(4,1)} %bitcast.315), calls=%async_computation.2 | async-start | bytes 7536640
  43.6 9.9 %collective-permute-start.2 = (bf16[2,2,104,384]{3,2,1,0:T(8,128)(2,1)S(1)}, bf16[2,2,104,384]{3,2,1,0:T(8,128)(2,1)S(1)}, u32[]{:S(2)}, u32[]{:S(2)}) collective-permute-start(bf16[2,2,104,384]{3,2,1,0:T(8,128)(2,1)S(1)} %bitcast.381), channel_id=1, source_target_pairs={{0,4},{4,8},{8,12},{1,5},{5,9},{9,13},{2,6},{6,10},{10,14},{3,7},{... | collective-permute-start | bytes 958472 | tf_op jit(solution)/shard_map/ppermute | solution.py:22
  53.6 3.9 %collective-permute-start.3 = (bf16[5,1,104,384]{3,2,1,0:T(8,128)(2,1)S(1)}, bf16[5,1,104,384]{3,2,1,0:T(8,128)(2,1)S(1)}, u32[]{:S(2)}, u32[]{:S(2)}) collective-permute-start(bf16[5,1,104,384]{3,2,1,0:T(8,128)(2,1)S(1)} %get-tuple-element.66), channel_id=1, source_target_pairs={{0,1},{1,2},{2,3},{4,5},{5,6},{6,7},{8,9},{9,10},{10,11},{12,13},{... | collective-permute-start | bytes 1198088 | tf_op jit(solution)/shard_map/ppermute | solution.py:30
  55.0 5.3 %collective-permute-start.4 = (bf16[5,1,104,384]{3,2,1,0:T(8,128)(2,1)S(1)}, bf16[5,1,104,384]{3,2,1,0:T(8,128)(2,1)S(1)}, u32[]{:S(2)}, u32[]{:S(2)}) collective-permute-start(bf16[5,1,104,384]{3,2,1,0:T(8,128)(2,1)S(1)} %get-tuple-element.67), channel_id=1, source_target_pairs={{1,0},{2,1},{3,2},{5,4},{6,5},{7,6},{9,8},{10,9},{11,10},{13,12},{... | collective-permute-start | bytes 1198088 | tf_op jit(solution)/shard_map/ppermute | solution.py:33
  75.7 1.2 copy-start.6
  75.7 6.9 %slice-start.2 = ((s8[7962624]{0:T(1024)(128)(4,1)}), s8[4194304]{0:T(1024)(128)(4,1)S(1)}, s32[]{:S(2)}) async-start(s8[7962624]{0:T(1024)(128)(4,1)} %bitcast.317), calls=%async_computation.3 | async-start | bytes 8388608
  76.3 5.7 %copy-start.8 = (bf16[384,384]{1,0:T(8,128)(2,1)S(1)}, bf16[384,384]{1,0:T(8,128)(2,1)}, u32[]{:S(2)}) copy-start(bf16[384,384]{1,0:T(8,128)(2,1)} %param.22) | copy-start | bytes 884740
  76.3 6.3 %slice-start.3 = ((s8[7962624]{0:T(1024)(128)(4,1)}), s8[3768320]{0:T(1024)(128)(4,1)S(1)}, s32[]{:S(2)}) async-start(s8[7962624]{0:T(1024)(128)(4,1)} %bitcast.317), calls=%async_computation.4 | async-start | bytes 7536640
  77.3 9.1 %collective-permute-start.5 = (bf16[2,2,104,384]{3,2,1,0:T(8,128)(2,1)S(1)}, bf16[2,2,104,384]{3,2,1,0:T(8,128)(2,1)S(1)}, u32[]{:S(2)}, u32[]{:S(2)}) collective-permute-start(bf16[2,2,104,384]{3,2,1,0:T(8,128)(2,1)S(1)} %bitcast.380), channel_id=1, source_target_pairs={{0,4},{4,8},{8,12},{1,5},{5,9},{9,13},{2,6},{6,10},{10,14},{3,7},{... | collective-permute-start | bytes 958472 | tf_op jit(solution)/shard_map/ppermute | solution.py:22
  86.5 9.5 %collective-permute-start.6 = (bf16[5,1,104,384]{3,2,1,0:T(8,128)(2,1)S(1)}, bf16[5,1,104,384]{3,2,1,0:T(8,128)(2,1)S(1)}, u32[]{:S(2)}, u32[]{:S(2)}) collective-permute-start(bf16[5,1,104,384]{3,2,1,0:T(8,128)(2,1)S(1)} %get-tuple-element.60), channel_id=1, source_target_pairs={{0,1},{1,2},{2,3},{4,5},{5,6},{6,7},{8,9},{9,10},{10,11},{12,13},{... | collective-permute-start | bytes 1198088 | tf_op jit(solution)/shard_map/ppermute | solution.py:30
  93.6 3.8 %collective-permute-start.7 = (bf16[5,1,104,384]{3,2,1,0:T(8,128)(2,1)S(1)}, bf16[5,1,104,384]{3,2,1,0:T(8,128)(2,1)S(1)}, u32[]{:S(2)}, u32[]{:S(2)}) collective-permute-start(bf16[5,1,104,384]{3,2,1,0:T(8,128)(2,1)S(1)} %get-tuple-element.61), channel_id=1, source_target_pairs={{1,0},{2,1},{3,2},{5,4},{6,5},{7,6},{9,8},{10,9},{11,10},{13,12},{... | collective-permute-start | bytes 1198088 | tf_op jit(solution)/shard_map/ppermute | solution.py:33
  113.2 1.1 copy-start.9
  114.2 3.8 %copy-start.3 = (bf16[624,384]{1,0:T(8,128)(2,1)}, bf16[624,384]{1,0:T(8,128)(2,1)S(1)}, u32[]{:S(2)}) copy-start(bf16[624,384]{1,0:T(8,128)(2,1)S(1)} %fusion.48) | copy-start | bytes 1437700
  116.2 144.8 %copy-start.1 = (bf16[384,384]{1,0:T(8,128)(2,1)S(1)}, bf16[384,384]{1,0:T(8,128)(2,1)}, u32[]{:S(2)}) copy-start(bf16[384,384]{1,0:T(8,128)(2,1)} %param.15) | copy-start | bytes 884740
Sparse Core Ops, SparseCore 0:
  118.2 138.7 all-reduce.4
